TPU v7x, 32 devices: a whole 2x2x4 slice. The times are simulated.
32 devices in a mesh: group: 4 (over x, core), shard: 8 (over z, y).
Axes of the slice: x: 2, y: 2, z: 4, core: 2. Of those that a mesh axis runs over, the one named last changes fastest.
Arguments:
- hidden: bfloat16 [8192, 768], P(('group', 'shard')), may hold values from -40 to 40
- out_grads: bfloat16 [5, 8192, 768], P(None, ('group', 'shard')), may hold values from -40 to 40
- global_inputs: bfloat16 [1024, 768], P(('group', 'shard')), may hold values from -40 to 40
- query_grads: bfloat16 [1024, 768], P(('group', 'shard')), may hold values from -40 to 40
- weight_grads: bfloat16 [6, 768, 768], P(None, 'shard'), may hold values from -48 to 48
- momentum: float32 [6, 768, 768], P(None, 'shard', 'group'), may hold values from -6 to 6
Outputs:
- new_momentum: float32 [6, 768, 768], P(None, 'shard', 'group')
All inputs are finite; a program needn't handle non-finite values. Where the computation divides by a largest or mean magnitude, that divisor is 1e-20 or more.
Results may differ from a plain program's by a relative error of at most 0.0018.
Values may be sent and summed in bfloat16 or wider, within the bound.
A program may use at most 128 MiB of HBM per device.

v0:
```python
import jax
import jax.numpy as jnp
from jax import lax
from jax.sharding import PartitionSpec as P

ITERS = 3


PRECISE = lax.Precision.HIGHEST
DAMPING = 0.1
MOMENTUM = 0.9


def broadcast(array, axis, root):
    mine = lax.axis_index(axis) == root
    return lax.psum(jnp.where(mine, array, jnp.zeros_like(array)), axis)


def outer_sum(matrix_rows):
    return lax.dot_general(
        matrix_rows, matrix_rows, (((0,), (0,)), ((), ())), preferred_element_type=jnp.float32
    )


def on_device(hidden, out_grads, global_inputs, query_grads, weight_grads, momentum):
    model_width = hidden.shape[1]
    group_size = lax.axis_size("group")
    shard_size = lax.axis_size("shard")
    per_group = 8 // group_size
    row_block = model_width // shard_size
    col_block = momentum.shape[2]
    shard_pos = lax.axis_index("shard")
    group_pos = lax.axis_index("group")
    devices = group_size * shard_size
    partials = [outer_sum(hidden), outer_sum(global_inputs)]
    partials = partials + [outer_sum(out_grads[member]) for member in range(5)]
    partials = partials + [outer_sum(query_grads)]
    stacked = jnp.stack([single.astype(jnp.bfloat16) for single in partials])
    summed = lax.psum_scatter(stacked, "group", scatter_dimension=0, tiled=True).astype(jnp.float32)
    factor_ids = group_pos * per_group + jnp.arange(per_group)
    is_global = (factor_ids == 1) | (factor_ids == 7)
    samp_total = float(hidden.shape[0] * devices)
    glob_total = float(global_inputs.shape[0] * devices)
    counted = jnp.where(is_global, glob_total, samp_total).astype(jnp.float32)
    factor_full = lax.psum(summed, "shard")
    covariance = factor_full / counted[:, None, None]
    mean_diag = jnp.trace(covariance, axis1=1, axis2=2) / model_width
    eye_full = jnp.eye(model_width, dtype=jnp.float32)
    matrix = covariance / mean_diag[:, None, None] + DAMPING * eye_full
    row_limit = jnp.max(jnp.sum(jnp.abs(matrix), axis=2), axis=1)
    approx = jnp.broadcast_to(eye_full, matrix.shape) / row_limit[:, None, None]
    for iteration in range(ITERS):
        product = jnp.einsum("kij,kjl->kil", matrix, approx, precision=PRECISE)
        approx = 2.0 * approx - jnp.einsum("kij,kjl->kil", approx, product, precision=PRECISE)
    own_rows = lax.dynamic_slice_in_dim(approx, shard_pos * row_block, row_block, 1)
    all_rows = lax.all_gather(own_rows, "group", axis=0, tiled=True)
    input_inv = jnp.stack(
        [broadcast(approx[factor % per_group], "group", factor // per_group) for factor in range(2)]
    )
    input_cols = lax.dynamic_slice_in_dim(input_inv, group_pos * col_block, col_block, 2)
    out_inverse = all_rows[2:8]
    initial = jnp.zeros(out_inverse.shape, jnp.float32)
    gathered = lax.all_gather(weight_grads, "shard", axis=1, tiled=True)
    columns = lax.slice_in_dim(out_inverse, 0, gathered.shape[1], axis=2)
    left_side = initial + jnp.einsum(
        "wrn,wnd->wrd", columns, gathered.astype(jnp.float32), precision=PRECISE
    )
    local_part = jnp.einsum("wrd,de->wre", left_side[0:5], input_cols[0], precision=PRECISE)
    global_part = jnp.dot(left_side[5], input_cols[1], precision=PRECISE)[None]
    return MOMENTUM * momentum + jnp.concatenate([local_part, global_part], axis=0)


def solution(mesh):
    placed = (
        P(("group", "shard"), None),
        P(None, ("group", "shard"), None),
        P(("group", "shard"), None),
        P(("group", "shard"), None),
        P(None, "shard", None),
        P(None, "shard", "group"),
    )
    return jax.shard_map(
        on_device, mesh=mesh, in_specs=placed, out_specs=P(None, "shard", "group"), check_vma=False
    )
```

profile of v0, /device:TPU:13, one launch (start us, length us, event | category | flops | bytes accessed | tf_op | source)
XLA Modules:
  0.0 528.5 jit_solution(5312361933273675997)
XLA Ops:
  7.4 1.0 copy-done
  8.4 1.5 fusion.14
  9.9 2.4 fusion.10
  12.3 2.7 fusion.16
  15.0 1.6 fusion.18
  16.5 1.6 fusion.20
  18.1 1.6 fusion.22
  19.7 1.5 fusion.24
  21.2 1.6 fusion.12
  23.3 1.5 fusion.26
  24.8 77.7 %reduce-scatter.2.cloned.1.call-done = bf16[2,768,768]{2,1,0:T(8,128)(2,1)} async-done(((bf16[8,768,768]{2,1,0:T(8,128)(2,1)}), bf16[2,768,768]{2,1,0:T(8,128)(2,1)}) %reduce-scatter.2.cloned.1.call-update) | async-done | bytes 2359312 | tf_op jit(solution)/shard_map/reduce_scatter | solution.py:39
  102.5 186.2 %all-reduce.5 = f32[2,768,768]{2,1,0:T(8,128)} all-reduce(bf16[2,768,768]{2,1,0:T(8,128)(2,1)} %reduce-scatter.2.cloned.1.call-done), channel_id=1, replica_groups=mesh['group'=4,'shard'=8] {'shard'}, use_global_device_ids=true, to_apply=%region_1.2 | all-reduce | flops 1179648 | bytes 7077888 | tf_op jit(solution)/shard_map/psum | solution.py:45
  288.6 3.7 select_reduce_fusion
  292.4 3.0 abs_reduce_fusion
  295.5 15.6 %fusion.2 = f32[2,768,768]{2,1,0:T(8,128)S(1)} fusion(f32[2,768,768]{2,1,0:T(8,128)} %get-tuple-element.8, f32[2]{0:T(128)S(1)} %reduce_max.9, f32[768,768]{1,0:T(8,128)} %fusion.26), kind=kOutput, calls=%fused_computation.10 | convolution fusion | flops 10872815616 | bytes 11796488 | tf_op jit(solution)/shard_map/kij,kjl->kil/dot_general | solution.py:53
  311.2 13.0 %multiply_subtract_fusion.2 = f32[2,768,768]{2,1,0:T(8,128)S(1)} fusion(f32[2]{0:T(128)S(1)} %reduce_max.9, f32[768,768]{1,0:T(8,128)S(1)} %copy-done.4, f32[2,768,768]{2,1,0:T(8,128)S(1)} %fusion.2), kind=kOutput, calls=%fused_computation.4 | convolution fusion | flops 10876354560 | bytes 11796488 | tf_op jit(solution)/shard_map/kij,kjl->kil/dot_general | solution.py:54
  324.2 12.1 %fusion.40 = f32[2,768,768]{2,1,0:T(8,128)S(1)} fusion(f32[2,768,768]{2,1,0:T(8,128)S(1)} %bitcast.80, f32[2,768,768]{2,1,0:T(8,128)S(1)} %multiply_subtract_fusion.2), kind=kOutput, calls=%fused_computation.65 | convolution fusion | flops 10871635968 | bytes 14155776 | tf_op jit(solution)/shard_map/kij,kjl->kil/dot_general | solution.py:53
  336.3 12.5 %multiply_subtract_fusion.1 = f32[2,768,768]{2,1,0:T(8,128)S(1)} fusion(f32[2,768,768]{2,1,0:T(8,128)S(1)} %multiply_subtract_fusion.2, f32[2,768,768]{2,1,0:T(8,128)S(1)} %fusion.40), kind=kOutput, calls=%fused_computation.3 | convolution fusion | flops 10873995264 | bytes 14155776 | tf_op jit(solution)/shard_map/kij,kjl->kil/dot_general | solution.py:54
  348.8 12.3 %fusion.41 = f32[2,768,768]{2,1,0:T(8,128)S(1)} fusion(f32[2,768,768]{2,1,0:T(8,128)S(1)} %bitcast.80, f32[2,768,768]{2,1,0:T(8,128)S(1)} %multiply_subtract_fusion.1), kind=kOutput, calls=%fused_computation.66 | convolution fusion | flops 10871635968 | bytes 14155776 | tf_op jit(solution)/shard_map/kij,kjl->kil/dot_general | solution.py:53
  361.1 12.6 %multiply_subtract_fusion = f32[2,768,768]{2,1,0:T(8,128)S(1)} fusion(f32[2,768,768]{2,1,0:T(8,128)S(1)} %multiply_subtract_fusion.1, f32[2,768,768]{2,1,0:T(8,128)S(1)} %fusion.41), kind=kOutput, calls=%fused_computation.2 | convolution fusion | flops 10873995264 | bytes 14155776 | tf_op jit(solution)/shard_map/kij,kjl->kil/dot_general | solution.py:54
  373.7 2.6 slice_select_fusion
  376.3 1.0 copy-done.3
  377.4 0.5 all-gather.5.cloned.1.call-update
  378.0 1.9 constant_dynamic-slice_fusion
  379.9 90.4 %all-reduce.4.cloned.1.call-done = (f32[1,768,768]{2,1,0:T(8,128)}, f32[1,768,768]{2,1,0:T(8,128)}) async-done(((f32[1,768,768]{2,1,0:T(8,128)}, f32[1,768,768]{2,1,0:T(8,128)}), (f32[1,768,768]{2,1,0:T(8,128)}, f32[1,768,768]{2,1,0:T(8,128)})) %all-reduce.4.cloned.1.call-update) | async-done | bytes 4718608 | tf_op jit(solution)/shard_map/psum | solution.py:16
  470.4 2.1 fusion.8
  472.5 11.7 %all-gather.5.cloned.1.call-done = bf16[6,768,768]{2,1,0:T(8,128)(2,1)} async-done(((bf16[6,96,768]{2,1,0:T(8,128)(2,1)}), bf16[6,768,768]{2,1,0:T(8,128)(2,1)}) %all-gather.5.cloned.1.call-update) | async-done | bytes 7077904 | tf_op jit(solution)/shard_map/all_gather | solution.py:63
  484.2 26.9 %all-gather.3.cloned.1.call-done = f32[8,96,768]{2,1,0:T(8,128)} async-done(((f32[2,96,768]{2,1,0:T(8,128)}), f32[8,96,768]{2,1,0:T(8,128)}) %all-gather.3.cloned.1.call-update) | async-done | bytes 2359312 | tf_op jit(solution)/shard_map/all_gather | solution.py:56
  511.1 6.7 %fusion.42 = f32[6,96,768]{2,1,0:T(8,128)S(1)} fusion(f32[8,96,768]{2,1,0:T(8,128)} %all-gather.3.cloned.1.call-done, bf16[6,768,768]{2,1,0:T(8,128)(2,1)} %all-gather.5.cloned.1.call-done), kind=kOutput, calls=%fused_computation.67 | convolution fusion | flops 4076863488 | bytes 11206656 | tf_op jit(solution)/shard_map/wrn,wnd->wrd/dot_general | solution.py:65
  517.9 1.3 fusion.29
  519.2 0.5 convolution_bitcast_fusion
  519.7 0.9 maximum_add_fusion
  (31 shorter events, 0.8 us)
Async XLA Ops:
  7.4 1.0 copy-start
  7.4 7.6 %copy-start.7 = (bf16[5,256,768]{2,1,0:T(8,128)(2,1)S(1)}, bf16[5,256,768]{2,1,0:T(8,128)(2,1)}, u32[]{:S(2)}) copy-start(bf16[5,256,768]{2,1,0:T(8,128)(2,1)} %param.7) | copy-start | bytes 5898244
  7.4 95.1 %reduce-scatter.2.cloned.1.call-start = ((), (), s32[]{:S(2)}) async-start(), calls=%async_computation.1 | async-start | bytes 11796480 | tf_op jit(solution)/shard_map/reduce_scatter | solution.py:39
  12.3 8.9 %copy-start.6 = (bf16[32,768]{1,0:T(8,128)(2,1)S(1)}, bf16[32,768]{1,0:T(8,128)(2,1)}, u32[]{:S(2)}) copy-start(bf16[32,768]{1,0:T(8,128)(2,1)} %param.9) | copy-start | bytes 147460
  22.9 447.5 %all-reduce.4.cloned.1.call-start = ((), (), s32[]{:S(2)}) async-start(), calls=%async_computation.4 | async-start | bytes 9437184 | tf_op jit(solution)/shard_map/psum | solution.py:16
  288.6 3.8 copy-start.2
  295.5 15.6 %copy-start.4 = (f32[768,768]{1,0:T(8,128)S(1)}, f32[768,768]{1,0:T(8,128)}, u32[]{:S(2)}) copy-start(f32[768,768]{1,0:T(8,128)} %fusion.26) | copy-start | bytes 7077892
  295.5 28.7 %slice-start = ((s8[4718592]{0:T(1024)(128)(4,1)}), s8[4194304]{0:T(1024)(128)(4,1)S(1)}, s32[]{:S(2)}) async-start(s8[4718592]{0:T(1024)(128)(4,1)} %bitcast.79), calls=%async_computation.5 | async-start | bytes 8388608
  311.1 13.0 %slice-start.1 = ((s8[4718592]{0:T(1024)(128)(4,1)}), s8[524288]{0:T(1024)(128)(4,1)S(1)}, s32[]{:S(2)}) async-start(s8[4718592]{0:T(1024)(128)(4,1)} %bitcast.79), calls=%async_computation.6 | async-start | bytes 1048576
  373.7 3.6 copy-start.3
  377.4 106.8 %all-gather.5.cloned.1.call-start = ((), (), s32[]{:S(2)}) async-start(), calls=%async_computation.3 | async-start | bytes 7962624 | tf_op jit(solution)/shard_map/all_gather | solution.py:63
  377.9 133.2 %all-gather.3.cloned.1.call-start = ((), (), s32[]{:S(2)}) async-start(), calls=%async_computation.2 | async-start | bytes 2949120 | tf_op jit(solution)/shard_map/all_gather | solution.py:56
  472.5 47.3 %copy-start.5 = (f32[6,96,192]{2,1,0:T(8,128)S(1)}, f32[6,96,192]{2,1,0:T(8,128)}, u32[]{:S(2)}) copy-start(f32[6,96,192]{2,1,0:T(8,128)} %param.11) | copy-start | bytes 1327108
  511.1 9.5 %copy-start.1 = (bf16[256,768]{1,0:T(8,128)(2,1)S(1)}, bf16[256,768]{1,0:T(8,128)(2,1)}, u32[]{:S(2)}) copy-start(bf16[256,768]{1,0:T(8,128)(2,1)} %param.6) | copy-start | bytes 1179652
Sparse Core Ops, SparseCore 0:
  23.0 79.4 reduce-scatter.1
  377.5 92.8 all-reduce.3
Sparse Core Ops, SparseCore 1:
  380.0 104.1 all-gather.4
  485.6 25.4 all-gather.2
where the time goes:
time: 534 us; the launch traced here: 529 us
  waiting for transfers between devices  207 us (39%)
  blocking collectives  186 us (35%)
  matrix products  101 us (19%)
  between operations  15.5 us (3%)
  other arithmetic  14.3 us (3%)
    psum x1, blocking collectives, on_device(): factor_full = lax.psum(summed, 'shard')  186 us
    psum x1, waiting for transfers between devices, broadcast(): return lax.psum(jnp.where(mine, array, jnp.zeros_like(array)), axis)  90.4 us
    reduce_scatter x1, waiting for transfers between devices, on_device(): lax.psum_scatter(stacked, 'group', scatter_dimension=0, tiled=True)  77.7 us
    dot_general x3, matrix products, on_device(): product = jnp.einsum('kij,kjl->kil', matrix, approx, precision=PRECISE)  40 us
    dot_general x3, matrix products, on_device(): jnp.einsum('kij,kjl->kil', approx, product, precision=PRECISE)  38.1 us
    all_gather x1, waiting for transfers between devices, on_device(): all_rows = lax.all_gather(own_rows, 'group', axis=0, tiled=True)  26.9 us
    dot_general x8, matrix products, outer_sum(): lax.dot_general(matrix_rows, matrix_rows, (((0,), (0,)), ((), ())), prefe...  14.5 us
    all_gather x1, waiting for transfers between devices, on_device(): gathered = lax.all_gather(weight_grads, 'shard', axis=1, tiled=True)  11.7 us
  transfers between devices with their start and end apart: 4, of which 4 were waited for; matrix products, arithmetic and copies ran while one was open for 1% of the time, Pallas kernels for 0%

commit v1 on v0

--- a/solution.py
+++ b/solution.py
@@ -1,6 +1,8 @@
 import jax
 import jax.numpy as jnp
 from jax import lax
+from jax.experimental import pallas as pl
+from jax.experimental.pallas import tpu as pltpu
 from jax.sharding import PartitionSpec as P
 
 ITERS = 3
@@ -70,6 +72,320 @@
     return MOMENTUM * momentum + jnp.concatenate([local_part, global_part], axis=0)
 
 
+MESH = pl.DeviceIdType.MESH
+BLK = 256
+HALF = 768
+QUART = 192
+
+
+def position():
+    group, shard = lax.axis_index("group"), lax.axis_index("shard")
+    core, x = lax.rem(group, 2), group // 2
+    y, z = lax.rem(shard, 2), shard // 2
+    return group, shard, core, x, y, z
+
+
+def weight_of(core, y, x):
+    return core * (2 + 2 * y + x) + (1 - core) * y * x
+
+
+def greet(peers):
+    barrier = pltpu.get_barrier_semaphore()
+    for peer in peers:
+        pl.semaphore_signal(barrier, inc=1, device_id=peer, device_id_type=MESH)
+    pl.semaphore_wait(barrier, len(peers))
+
+
+def add_rows(store, loads, rows):
+    def step(i, carry):
+        at = pl.multiple_of(i * 64, 64)
+        total = loads[0](at).astype(jnp.float32)
+        for load in loads[1:]:
+            total = total + load(at).astype(jnp.float32)
+        store(at, total.astype(jnp.bfloat16))
+        return carry
+
+    lax.fori_loop(0, rows // 64, step, 0)
+
+
+def reduce_kernel(hid, ginp, outg, qry, wgr, cov, gfull, sendb, keep, rc, r2, r3, acc, zr,
+                  cs, cr, as_, ar, bs, br, zs, zrs, fs, fr, gs, gr, lsem):
+    group, shard, core, x, y, z = position()
+    sibling = (group + 1 - 2 * core, shard)
+    x_peer = ((1 - x) * 2 + core, shard)
+    y_peer = (group, 2 * z + 1 - y)
+    z_of = [lax.rem(z + dz, 4) for dz in range(4)]
+    y_of = [y, 1 - y]
+    shard_peers = [(dz, dy) for dz in range(4) for dy in range(2) if dz + dy > 0]
+    greet([sibling, x_peer] + [(group, 2 * z_of[dz] + y_of[dy]) for dz, dy in shard_peers])
+
+    def remote(src, dst, send, recv, device):
+        return pltpu.make_async_remote_copy(
+            src_ref=src, dst_ref=dst, send_sem=send, recv_sem=recv, device_id=device, device_id_type=MESH
+        )
+
+    def partial(factor, dst):
+        if factor == 0:
+            rows = hid[...]
+        elif factor == 1:
+            rows = ginp[...]
+        elif factor == 7:
+            rows = qry[...]
+        else:
+            rows = outg[factor - 2]
+        at = 0
+        for i in range(3):
+            prod = lax.dot_general(
+                rows[:, BLK * i:BLK * (i + 1)], rows[:, BLK * i:], (((0,), (0,)), ((), ())),
+                preferred_element_type=jnp.float32,
+            ).astype(jnp.bfloat16)
+            for j in range(3 - i):
+                dst[at * BLK:(at + 1) * BLK, :] = prod[:, BLK * j:BLK * (j + 1)]
+                at += 1
+
+    core_copies = [remote(sendb.at[j], rc.at[j], cs.at[j], cr.at[j], sibling) for j in range(4)]
+    for owner in range(2):
+        @pl.when(core != owner)
+        def _():
+            for j in range(4):
+                partial(4 * owner + j, sendb.at[j])
+                core_copies[j].start()
+
+    grad_copies = []
+    for k, (dz, dy) in enumerate(shard_peers):
+        copy = remote(wgr.at[weight_of(core, y_of[dy], x)], gfull.at[shard], gs.at[k], gr.at[k],
+                      (group, 2 * z_of[dz] + y_of[dy]))
+        copy.start()
+        grad_copies.append(copy)
+    local = pltpu.make_async_copy(wgr.at[weight_of(core, y, x)], gfull.at[shard], lsem)
+    local.start()
+    for owner in range(2):
+        @pl.when(core == owner)
+        def _():
+            for j in range(4):
+                partial(4 * owner + j, keep.at[j])
+
+    for j in range(4):
+        core_copies[j].wait()
+
+        def store(at, value, j=j):
+            keep[j, pl.ds(at, 64), :] = value
+
+        add_rows(store, [lambda at, j=j: keep[j, pl.ds(at, 64), :], lambda at, j=j: rc[j, pl.ds(at, 64), :]], 2 * HALF)
+
+    first = [remote(keep.at[2 * t + 1 - x, pl.ds(0, HALF)], r2.at[0, t], as_.at[t], ar.at[t], x_peer) for t in range(2)]
+    first += [remote(keep.at[2 * (1 - y) + t, pl.ds(HALF, HALF)], r2.at[1, t], as_.at[2 + t], ar.at[2 + t], y_peer)
+              for t in range(2)]
+    for copy in (first[0], first[2], first[1], first[3]):
+        copy.start()
+    for copy in first:
+        copy.wait()
+    passed = [2 * (1 - y) + x, 2 * y + 1 - x]
+    other = [1 - y, 1 - x]
+    same = [y, x]
+    second = [remote(keep.at[passed[h], pl.ds(h * HALF, HALF)], r3.at[h], bs.at[h], br.at[h], [y_peer, x_peer][h])
+              for h in range(2)]
+    for h in range(2):
+        def store(at, value, h=h):
+            keep[passed[h], pl.ds(h * HALF + at, 64), :] = value
+
+        add_rows(store, [lambda at, h=h: keep[passed[h], pl.ds(h * HALF + at, 64), :],
+                         lambda at, h=h: r2[h, other[h], pl.ds(at, 64), :]], HALF)
+        second[h].start()
+    mine = 2 * y + x
+    scatter, gather = [], []
+    for h in range(2):
+        second[h].wait()
+
+        def store(at, value, h=h):
+            acc[pl.ds(h * HALF + at, 64), :] = value
+
+        add_rows(store, [lambda at, h=h: keep[mine, pl.ds(h * HALF + at, 64), :],
+                         lambda at, h=h: r2[h, same[h], pl.ds(at, 64), :],
+                         lambda at, h=h: r3[h, pl.ds(at, 64), :]], HALF)
+        for dz in range(1, 4):
+            copy = remote(acc.at[pl.ds(h * HALF + z_of[dz] * QUART, QUART)], zr.at[h, dz - 1],
+                          zs.at[h, dz - 1], zrs.at[h, dz - 1], (group, 2 * z_of[dz] + y))
+            copy.start()
+            scatter.append(copy)
+    for h in range(2):
+        for copy in scatter[3 * h:3 * h + 3]:
+            copy.wait()
+        base = h * HALF + z * QUART
+
+        def store(at, value, base=base):
+            cov[pl.ds(base + at, 64), :] = value
+
+        loads = [lambda at, base=base: acc[pl.ds(base + at, 64), :]]
+        loads += [lambda at, h=h, d=d: zr[h, d, pl.ds(at, 64), :] for d in range(3)]
+        add_rows(store, loads, QUART)
+        for dz in range(1, 4):
+            copy = remote(cov.at[pl.ds(base, QUART)], cov.at[pl.ds(base, QUART)],
+                          fs.at[h, dz - 1], fr.at[h, dz - 1], (group, 2 * z_of[dz] + y))
+            copy.start()
+            gather.append(copy)
+    for copy in gather + grad_copies:
+        copy.wait()
+    local.wait()
+
+
+def spread_kernel(lch, xch, lout, xout, ls, lr, lsem):
+    group, shard, core, x, y, z = position()
+    offsets = [(dg, dy) for dg in range(4) for dy in range(2)]
+    peers = [(lax.rem(group + dg, 4), lax.rem(y + dy, 2)) for dg, dy in offsets]
+    greet([(pg, 2 * z + py) for pg, py in peers[1:]])
+    weight = weight_of(core, y, x)
+
+    def remote_left(k):
+        pg, py = peers[k]
+        return pltpu.make_async_remote_copy(
+            src_ref=lch.at[py], dst_ref=lout.at[weight], send_sem=ls.at[k], recv_sem=lr.at[k],
+            device_id=(pg, 2 * z + py), device_id_type=MESH)
+
+    def remote_input(k):
+        pg, py = peers[k]
+        return pltpu.make_async_remote_copy(
+            src_ref=xch.at[pg], dst_ref=xout.at[x], send_sem=ls.at[k], recv_sem=lr.at[k],
+            device_id=(pg, 2 * z + py), device_id_type=MESH)
+
+    @pl.when(core + y > 0)
+    def _():
+        for k in range(1, 8):
+            remote_left(k).start()
+        local = pltpu.make_async_copy(lch.at[y], lout.at[weight], lsem)
+        local.start()
+        local.wait()
+        for k in range(1, 8):
+            remote_left(k).wait_send()
+
+    @pl.when(core + y == 0)
+    def _():
+        for k in range(1, 8):
+            remote_input(k).start()
+        local = pltpu.make_async_copy(xch.at[group], xout.at[x], lsem)
+        local.start()
+        local.wait()
+        for k in range(1, 8):
+            remote_input(k).wait_send()
+
+    for k in range(1, 8):
+        dg, dy = offsets[k]
+        from_core = lax.rem(lax.rem(group + 4 - dg, 4), 2)
+        from_y = lax.rem(y + dy, 2)
+
+        @pl.when(from_core + from_y > 0)
+        def _():
+            remote_left(k).wait_recv()
+
+        @pl.when(from_core + from_y == 0)
+        def _():
+            remote_input(k).wait_recv()
+
+
+def split_high(values):
+    high = lax.reduce_precision(values, 8, 7)
+    return high.astype(jnp.bfloat16), (values - high).astype(jnp.bfloat16)
+
+
+def fast_device(hidden, out_grads, global_inputs, query_grads, weight_grads, momentum):
+    width = hidden.shape[1]
+    group, shard, core, x, y, z = position()
+    vmem = pl.BlockSpec(memory_space=pltpu.VMEM)
+    dma = pltpu.SemaphoreType.DMA
+    bf16 = jnp.bfloat16
+    packed, gfull = pl.pallas_call(
+        reduce_kernel,
+        out_shape=(jax.ShapeDtypeStruct((2 * HALF, BLK), bf16), jax.ShapeDtypeStruct((8, 96, width), bf16)),
+        in_specs=[vmem] * 5,
+        out_specs=(vmem, vmem),
+        scratch_shapes=[
+            pltpu.VMEM((4, 2 * HALF, BLK), bf16),
+            pltpu.VMEM((4, 2 * HALF, BLK), bf16),
+            pltpu.VMEM((4, 2 * HALF, BLK), bf16),
+            pltpu.VMEM((2, 2, HALF, BLK), bf16),
+            pltpu.VMEM((2, HALF, BLK), bf16),
+            pltpu.VMEM((2 * HALF, BLK), bf16),
+            pltpu.VMEM((2, 3, QUART, BLK), bf16),
+            dma((4,)), dma((4,)), dma((4,)), dma((4,)), dma((2,)), dma((2,)),
+            dma((2, 3)), dma((2, 3)), dma((2, 3)), dma((2, 3)), dma((7,)), dma((7,)), dma,
+        ],
+        compiler_params=pltpu.CompilerParams(collective_id=0, has_side_effects=True, vmem_limit_bytes=48 * 2**20),
+    )(hidden, global_inputs, out_grads, query_grads, weight_grads)
+    blocks = packed.reshape(6, BLK, BLK).astype(jnp.float32)
+    b00, b01, b02, b11, b12, b22 = [blocks[i] for i in range(6)]
+    total = jnp.concatenate([
+        jnp.concatenate([b00, b01, b02], axis=1),
+        jnp.concatenate([b01.T, b11, b12], axis=1),
+        jnp.concatenate([b02.T, b12.T, b22], axis=1),
+    ], axis=0)
+    devices = lax.axis_size("group") * lax.axis_size("shard")
+    factor = 4 * core + 2 * y + x
+    is_global = (factor == 1) | (factor == 7)
+    counted = jnp.where(is_global, float(global_inputs.shape[0] * devices), float(hidden.shape[0] * devices))
+    covariance = total / counted.astype(jnp.float32)
+    eye = jnp.eye(width, dtype=jnp.float32)
+    mean_diag = jnp.trace(covariance) / width
+    matrix = covariance / mean_diag + DAMPING * eye
+    row_limit = jnp.max(jnp.sum(jnp.abs(matrix), axis=1))
+    a1 = matrix / row_limit
+
+    def mul(left, right):
+        return jnp.dot(left, right, precision=lax.Precision.HIGH)
+
+    a2 = mul(a1, a1)
+    a3 = mul(a1, a2)
+    a4 = mul(a2, a2)
+    rest = 4.0 * a2 - 6.0 * a1 - a3
+    prod = 4.0 * a1 - 6.0 * a2 + 4.0 * a3 - a4
+    inverse = (8.0 * eye + 2.0 * rest - 4.0 * prod - mul(rest, prod)) / row_limit
+    diag = jnp.sum(inverse * eye, axis=1)
+    off = (inverse * (1.0 - eye)).astype(bf16)
+    grads = gfull.reshape(width, width)
+    left = jnp.dot(lax.dynamic_slice_in_dim(off, z * 2 * 96, 2 * 96, 0), grads, preferred_element_type=jnp.float32)
+    high, low = split_high(diag)
+
+    def with_diag(rows, size):
+        extra = jnp.zeros((rows.shape[0], 16, width), bf16)
+        extra = extra.at[:, 0, :size].set(high_of(size)).at[:, 1, :size].set(low_of(size))
+        return jnp.concatenate([rows, extra], axis=1)
+
+    def high_of(size):
+        if size == 96:
+            return lax.dynamic_slice_in_dim(high, z * 192, 192, 0).reshape(2, 96)
+        return high.reshape(4, 192)
+
+    def low_of(size):
+        if size == 96:
+            return lax.dynamic_slice_in_dim(low, z * 192, 192, 0).reshape(2, 96)
+        return low.reshape(4, 192)
+
+    left_chunks = with_diag(left.astype(bf16).reshape(2, 96, width), 96)
+    input_chunks = with_diag(off.reshape(4, 192, width), 192)
+    left_all, input_all = pl.pallas_call(
+        spread_kernel,
+        out_shape=(jax.ShapeDtypeStruct((6, 112, width), bf16), jax.ShapeDtypeStruct((2, 208, width), bf16)),
+        in_specs=[vmem] * 2,
+        out_specs=(vmem, vmem),
+        scratch_shapes=[dma((8,)), dma((8,)), dma],
+        compiler_params=pltpu.CompilerParams(collective_id=1, has_side_effects=True, vmem_limit_bytes=32 * 2**20),
+    )(left_chunks, input_chunks)
+    out_diag = left_all[:, 96, :96].astype(jnp.float32) + left_all[:, 97, :96].astype(jnp.float32)
+    left_side = out_diag[:, :, None] * weight_grads.astype(jnp.float32) + left_all[:, :96].astype(jnp.float32)
+    in_diag = input_all[:, 192, :192].astype(jnp.float32) + input_all[:, 193, :192].astype(jnp.float32)
+    columns = lax.dynamic_slice_in_dim(left_side, group * 192, 192, 2)
+    narrow = left_side.astype(bf16)
+
+    def right(rows, which):
+        return lax.dot_general(rows, input_all[which, :192], (((rows.ndim - 1,), (1,)), ((), ())),
+                               preferred_element_type=jnp.float32)
+
+    step = jnp.concatenate([
+        right(narrow[0:5], 0) + columns[0:5] * in_diag[0],
+        (right(narrow[5], 1) + columns[5] * in_diag[1])[None],
+    ], axis=0)
+    return MOMENTUM * momentum + step
+
+
 def solution(mesh):
     placed = (
         P(("group", "shard"), None),
@@ -79,6 +395,7 @@
         P(None, "shard", None),
         P(None, "shard", "group"),
     )
+    pairs = mesh.shape["group"] == 4 and mesh.shape["shard"] == 8
     return jax.shard_map(
-        on_device, mesh=mesh, in_specs=placed, out_specs=P(None, "shard", "group"), check_vma=False
+        fast_device if pairs else on_device, mesh=mesh, in_specs=placed, out_specs=P(None, "shard", "group"), check_vma=False
     )

time: 534 us -> 143 us (0.27)
  waiting for transfers between devices: 207 us -> 0 us
  blocking collectives: 186 us -> 0 us
  Pallas kernels: 0 us -> 107 us
  matrix products: 101 us -> 19.6 us
  between operations: 15.5 us -> 0.94 us
  other arithmetic: 14.3 us -> 5.77 us
    psum x1 -> x0, blocking collectives: 186 us -> none  [on_device(): factor_full = lax.psum(summed, 'shard')]
    pallas_call x0 -> x2, Pallas kernels: none -> 107 us  [the longest x1 82.2 us: fast_device(): pl.pallas_call(reduce_kernel, out_shape=(jax.ShapeDtypeStruct((2 * HALF,...]
    psum x1 -> x0, waiting for transfers between devices: 90.4 us -> none  [broadcast(): return lax.psum(jnp.where(mine, array, jnp.zeros_like(array)), axis)]
    dot_general x17 -> x7, matrix products: 101 us -> 19.6 us  [the longest x4 18.5 us: mul(): return jnp.dot(left, right, precision=lax.Precision.HIGH)]
    reduce_scatter x1 -> x0, waiting for transfers between devices: 77.7 us -> none  [on_device(): lax.psum_scatter(stacked, 'group', scatter_dimension=0, tiled=True)]
    all_gather x2 -> x0, waiting for transfers between devices: 38.7 us -> none  [the longest x1 26.9 us: on_device(): all_rows = lax.all_gather(own_rows, 'group', axis=0, tiled=True)]
  transfers between devices with their start and end apart: 4 -> 0, of which waited for: 4 -> 0; matrix products, arithmetic and copies ran while one was open for 1% -> 0% of each run, Pallas kernels for 0% -> 0%
where the time goes in v1:
time: 143 us
  Pallas kernels  107 us (75%)
  matrix products  19.6 us (14%)
  local copies, waits for them, and re-layouts  9.07 us (6%)
  other arithmetic  5.77 us (4%)
    pallas_call x1, Pallas kernels, fast_device(): pl.pallas_call(reduce_kernel, out_shape=(jax.ShapeDtypeStruct((2 * HALF,...  82.2 us
    pallas_call x1, Pallas kernels, fast_device(): pl.pallas_call(spread_kernel, out_shape=(jax.ShapeDtypeStruct((6, 112, wi...  25.1 us
    dot_general x4, matrix products, mul(): return jnp.dot(left, right, precision=lax.Precision.HIGH)  18.5 us
    unnamed x26, local copies, waits for them, and re-layouts  6.13 us

profile of v1, /device:TPU:13, one launch (start us, length us, event | category | flops | bytes accessed | tf_op | source)
XLA Modules:
  0.0 142.6 jit_solution(7982355469887656698)
XLA Ops:
  0.0 1.2 copy-done
  1.2 1.5 %copy-done.2 = bf16[5,256,768]{2,1,0:T(8,128)(2,1)S(1)} copy-done((bf16[5,256,768]{2,1,0:T(8,128)(2,1)S(1)}, bf16[5,256,768]{2,1,0:T(8,128)(2,1)}, u32[]{:S(2)}) %copy-start.2) | copy-done | bytes 1966104
  2.7 1.0 copy-done.3
  3.7 0.8 copy-done.4
  4.5 0.8 copy-done.5
  5.3 82.2 %shard_map.64 = (bf16[1536,256]{1,0:T(8,128)(2,1)S(1)}, bf16[8,96,768]{2,1,0:T(8,128)(2,1)S(1)}) custom-call(bf16[256,768]{1,0:T(8,128)(2,1)S(1)} %copy-done.3, bf16[32,768]{1,0:T(8,128)(2,1)S(1)} %copy-done.4, bf16[5,256,768]{2,1,0:T(8,128)(2,1)S(1)} %copy-done.2, bf16[32,768]{1,0:T(8,128)(2,1)S(1)} %copy-done.5, bf16[6,96,768]{2,1,0:T(8,128)(2,1)S(1)} %copy-done), custom_call_target="tpu_custom_call" | custom-call | tf_op jit(solution)/shard_map/pallas_call | solution.py:296
  87.5 0.1 convert_element_type.71
  87.6 0.8 copy.15
  88.5 0.9 fusion.17
  89.4 0.1 copy.20
  89.6 0.1 copy.21
  89.7 0.1 copy.22
  89.9 0.3 copy.16
  90.2 1.9 %select_reduce_fusion.1 = f32[]{:T(128)} fusion(f32[]{:T(128)S(6)} %select_n.26, f32[256,256]{1,0:T(8,128)} %get-tuple-element.72, f32[256,256]{1,0:T(8,128)} %copy.15, f32[256,256]{1,0:T(8,128)S(1)} %bitcast.38, f32[256,256]{1,0:T(8,128)} %get-tuple-element.70, f32[256,256]{1,0:T(8,128)S(1)} %get-tuple-element.69, f32[256,256]{1,0:T(8,128)S(1)} %bitcast.36, ...), kind=kLoop, calls=%fused_computation.8 | loop fusion | flops 5898239 | bytes 2359304 | tf_op jit(solution)/shard_map/jit(trace)/reduce_sum | solution.py:327
  92.8 1.7 %abs_reduce_fusion = (f32[768]{0:T(1024)S(1)}, f32[768,768]{1,0:T(8,128)}) fusion(f32[]{:T(128)S(6)} %multiply.7, f32[256,256]{1,0:T(8,128)S(1)} %copy-done.7, f32[256,256]{1,0:T(8,128)S(1)} %copy-done.8, f32[256,256]{1,0:T(8,128)S(1)} %bitcast.39, f32[256,256]{1,0:T(8,128)S(1)} %copy-done.6, f32[256,256]{1,0:T(8,128)S(1)} %get-tuple-element.69, ...), kind=kLoop, calls=%fused_computation.6 | loop fusion | flops 7077120 | bytes 4721668 | tf_op jit(solution)/shard_map/reduce_sum | solution.py:329
  94.5 0.6 reduce_max.9
  95.1 6.1 %fusion.15 = f32[768,768]{1,0:T(8,128)S(1)} fusion(f32[768,768]{1,0:T(8,128)} %get-tuple-element.64, f32[]{:T(128)} %reduce_max.9), kind=kOutput, calls=%fused_computation.45 | convolution fusion | flops 2718498816 | bytes 4718596 | tf_op jit(solution)/shard_map/dot_general | solution.py:333
  101.2 3.1 %fusion.19 = f32[768,768]{1,0:T(8,128)S(1)} fusion(f32[768,768]{1,0:T(8,128)S(1)} %fusion.15), kind=kOutput, calls=%fused_computation.49 | convolution fusion | flops 2717908992 | bytes 4718592 | tf_op jit(solution)/shard_map/dot_general | solution.py:333
  104.4 3.8 %fusion.14 = f32[768,768]{1,0:T(8,128)S(1)} fusion(f32[768,768]{1,0:T(8,128)S(1)} %fusion.15, f32[768,768]{1,0:T(8,128)S(1)} %copy-done.9, f32[]{:T(128)} %reduce_max.9), kind=kOutput, calls=%fused_computation.44 | convolution fusion | flops 2718498816 | bytes 7077892 | tf_op jit(solution)/shard_map/dot_general | solution.py:333
  108.2 5.5 %multiply_convert_fusion = (bf16[768,768]{1,0:T(8,128)(2,1)S(1)}, f32[768]{0:T(1024)S(1)}) fusion(f32[768,768]{1,0:T(8,128)S(1)} %fusion.19, f32[768,768]{1,0:T(8,128)S(1)} %fusion.14, f32[768,768]{1,0:T(8,128)S(1)} %fusion.15, f32[768,768]{1,0:T(8,128)S(1)} %copy-done.9, f32[]{:T(128)} %reduce_max.9), kind=kOutput, calls=%fused_computation.2 | convolution fusion | flops 2739731712 | bytes 10619908 | tf_op jit(solution)/shard_map/dot_general | solution.py:333
  113.7 0.4 convolution_convert_fusion
  114.3 0.1 reshape.223
  114.4 0.1 reshape.224
  114.5 0.2 scatter.15
  114.8 0.3 scatter.19
  115.1 0.1 pad_maximum_fusion.xch
  115.1 25.1 %shard_map.65 = (bf16[6,112,768]{2,1,0:T(8,128)(2,1)S(1)}, bf16[2,208,768]{2,1,0:T(8,128)(2,1)S(1)}) custom-call(bf16[2,112,768]{2,1,0:T(8,128)(2,1)S(1)} %pad_maximum_fusion.2.lch, bf16[4,208,768]{2,1,0:T(8,128)(2,1)S(1)} %pad_maximum_fusion.xch), custom_call_target="tpu_custom_call" | custom-call | tf_op jit(solution)/shard_map/pallas_call | solution.py:364
  140.3 0.3 fusion.16
  140.6 0.2 fusion.2
  140.9 0.4 convolution_add_fusion
  141.3 0.4 copy-done.10
  141.7 0.9 maximum_add_fusion
  (30 shorter events, 0.4 us)
Async XLA Ops:
  0.0 1.2 copy-start
  1.2 1.5 %copy-start.2 = (bf16[5,256,768]{2,1,0:T(8,128)(2,1)S(1)}, bf16[5,256,768]{2,1,0:T(8,128)(2,1)}, u32[]{:S(2)}) copy-start(bf16[5,256,768]{2,1,0:T(8,128)(2,1)} %outg.1) | copy-start | bytes 5898244
  2.7 1.0 copy-start.3
  3.7 0.8 copy-start.4
  4.5 0.8 copy-start.5
  90.2 2.6 %copy-start.6 = (f32[256,256]{1,0:T(8,128)S(1)}, f32[256,256]{1,0:T(8,128)}, u32[]{:S(2)}) copy-start(f32[256,256]{1,0:T(8,128)} %get-tuple-element.70) | copy-start | bytes 786436
  90.2 2.6 %copy-start.7 = (f32[256,256]{1,0:T(8,128)S(1)}, f32[256,256]{1,0:T(8,128)}, u32[]{:S(2)}) copy-start(f32[256,256]{1,0:T(8,128)} %get-tuple-element.72) | copy-start | bytes 786436
  90.2 2.6 %copy-start.8 = (f32[256,256]{1,0:T(8,128)S(1)}, f32[256,256]{1,0:T(8,128)}, u32[]{:S(2)}) copy-start(f32[256,256]{1,0:T(8,128)} %copy.15) | copy-start | bytes 786436
  101.2 3.2 %copy-start.9 = (f32[768,768]{1,0:T(8,128)S(1)}, f32[768,768]{1,0:T(8,128)}, u32[]{:S(2)}) copy-start(f32[768,768]{1,0:T(8,128)} %get-tuple-element.64) | copy-start | bytes 7077892
  114.7 25.6 %copy-start.1 = (bf16[6,96,768]{2,1,0:T(8,128)(2,1)S(1)}, bf16[6,96,768]{2,1,0:T(8,128)(2,1)}, u32[]{:S(2)}) copy-start(bf16[6,96,768]{2,1,0:T(8,128)(2,1)} %wgr.1) | copy-start | bytes 2654212
  140.6 1.1 copy-start.10

commit v2 on v0

--- a/solution.py
+++ b/solution.py
@@ -1,6 +1,8 @@
 import jax
 import jax.numpy as jnp
 from jax import lax
+from jax.experimental import pallas as pl
+from jax.experimental.pallas import tpu as pltpu
 from jax.sharding import PartitionSpec as P
 
 ITERS = 3
@@ -70,6 +72,391 @@
     return MOMENTUM * momentum + jnp.concatenate([local_part, global_part], axis=0)
 
 
+MESH = pl.DeviceIdType.MESH
+BLK = 256
+HALF = 768
+PARTS = 2
+SUB = HALF // PARTS
+ZROWS = SUB // 4
+STEP = 32
+
+
+def position():
+    group, shard = lax.axis_index("group"), lax.axis_index("shard")
+    core, x = lax.rem(group, 2), group // 2
+    y, z = lax.rem(shard, 2), shard // 2
+    return group, shard, core, x, y, z
+
+
+def weight_of(core, y, x):
+    return core * (2 + 2 * y + x) + (1 - core) * y * x
+
+
+def greet(peers):
+    barrier = pltpu.get_barrier_semaphore()
+    for peer in peers:
+        pl.semaphore_signal(barrier, inc=1, device_id=peer, device_id_type=MESH)
+    pl.semaphore_wait(barrier, len(peers))
+
+
+def add_rows(store, loads, rows):
+    def step(i, carry):
+        at = pl.multiple_of(i * STEP, STEP)
+        total = loads[0](at).astype(jnp.float32)
+        for load in loads[1:]:
+            total = total + load(at).astype(jnp.float32)
+        store(at, total.astype(jnp.bfloat16))
+        return carry
+
+    lax.fori_loop(0, rows // STEP, step, 0)
+
+
+def step_kernel(hid, ginp, outg, qry, wgr, lout, xout, dall, sendb, keep, rc, r2, r3, acc, zr,
+                cov, gfull, off_a, off_b, off_r, off_y, nar_a, nar_b, nar_r, nar_y, left,
+                cs, cr, as_, ar, bs, br, zs, zrs, fs, fr, gs, gr, ls, lr, ds_, dr, lsem, lsem2, dsem):
+    group, shard, core, x, y, z = position()
+    sibling = (group + 1 - 2 * core, shard)
+    x_peer = ((1 - x) * 2 + core, shard)
+    y_peer = (group, 2 * z + 1 - y)
+    z_of = [lax.rem(z + dz, 4) for dz in range(4)]
+    y_of = [y, 1 - y]
+    shard_peers = [(dz, dy) for dz in range(4) for dy in range(2) if dz + dy > 0]
+    plane = [(dg, dy) for dg in range(4) for dy in range(2) if dg + dy > 0]
+    plane_to = [(lax.rem(group + dg, 4), y_of[dy]) for dg, dy in plane]
+    plane_from = [(lax.rem(group + 4 - dg, 4), y_of[dy]) for dg, dy in plane]
+    outside = [(pg, 2 * z + py) for (pg, py), (dg, dy) in zip(plane_to, plane) if dg > 0]
+    greet(outside + [(group, 2 * z_of[dz] + y_of[dy]) for dz, dy in shard_peers])
+
+    def remote(src, dst, send, recv, device):
+        return pltpu.make_async_remote_copy(
+            src_ref=src, dst_ref=dst, send_sem=send, recv_sem=recv, device_id=device, device_id_type=MESH
+        )
+
+    def partial(factor, dst):
+        if factor == 0:
+            rows = hid[...]
+        elif factor == 1:
+            rows = ginp[...]
+        elif factor == 7:
+            rows = qry[...]
+        else:
+            rows = outg[factor - 2]
+        at = 0
+        for i in range(3):
+            prod = lax.dot_general(
+                rows[:, BLK * i:BLK * (i + 1)], rows[:, BLK * i:], (((0,), (0,)), ((), ())),
+                preferred_element_type=jnp.float32,
+            ).astype(jnp.bfloat16)
+            for j in range(3 - i):
+                dst[at * BLK:(at + 1) * BLK, :] = prod[:, BLK * j:BLK * (j + 1)]
+                at += 1
+
+    grad_copies = []
+    for i, (dz, dy) in enumerate(shard_peers):
+        grad_copies.append(remote(wgr.at[weight_of(core, y_of[dy], x)], gfull.at[pl.ds(shard * 96, 96)], gs.at[i],
+                                  gr.at[i], (group, 2 * z_of[dz] + y_of[dy])))
+
+        @pl.when(core + y_of[dy] > 0)
+        def _(copy=grad_copies[-1]):
+            copy.start()
+
+    local = pltpu.make_async_copy(wgr.at[weight_of(core, y, x)], gfull.at[pl.ds(shard * 96, 96)], lsem)
+    local.start()
+    core_copies = [remote(sendb.at[j], rc.at[j], cs.at[j], cr.at[j], sibling) for j in range(4)]
+    for owner in range(2):
+        @pl.when(core != owner)
+        def _():
+            for j in range(4):
+                partial(4 * owner + j, sendb.at[j])
+                core_copies[j].start()
+
+    for owner in range(2):
+        @pl.when(core == owner)
+        def _():
+            for j in range(4):
+                partial(4 * owner + j, keep.at[j])
+
+    for j in range(4):
+        core_copies[j].wait()
+
+    def first_of(h, q):
+        rows = pl.ds(h * HALF + q * SUB, SUB)
+        into = pl.ds(q * SUB, SUB)
+        if h == 0:
+            return [remote(keep.at[2 * t + 1 - x, rows], r2.at[0, t, into], as_.at[h, q, t], ar.at[h, q, t], x_peer)
+                    for t in range(2)]
+        return [remote(keep.at[2 * (1 - y) + t, rows], r2.at[1, t, into], as_.at[h, q, t], ar.at[h, q, t], y_peer)
+                for t in range(2)]
+
+    passed = [2 * (1 - y) + x, 2 * y + 1 - x]
+    other = [1 - y, 1 - x]
+    same = [y, x]
+    mine = 2 * y + x
+    halves = [(h, q) for q in range(PARTS) for h in range(2)]
+    first = {hq: first_of(*hq) for hq in halves}
+    second = {(h, q): remote(keep.at[passed[h], pl.ds(h * HALF + q * SUB, SUB)], r3.at[h, pl.ds(q * SUB, SUB)],
+                             bs.at[h, q], br.at[h, q], [y_peer, x_peer][h]) for h, q in halves}
+
+    def own_rows(h, q):
+        return h * HALF + q * SUB + z * ZROWS
+
+    def scatter_of(h, q):
+        return [remote(acc.at[pl.ds(h * HALF + q * SUB + z_of[dz] * ZROWS, ZROWS)], zr.at[h, q, dz - 1],
+                       zs.at[h, q, dz - 1], zrs.at[h, q, dz - 1], (group, 2 * z_of[dz] + y)) for dz in range(1, 4)]
+
+    def gather_of(h, q):
+        rows = pl.ds(own_rows(h, q), ZROWS)
+        return [remote(cov.at[rows], cov.at[rows], fs.at[h, q, dz - 1], fr.at[h, q, dz - 1],
+                       (group, 2 * z_of[dz] + y)) for dz in range(1, 4)]
+
+    scatter = {hq: scatter_of(*hq) for hq in halves}
+    gather = {hq: gather_of(*hq) for hq in halves}
+
+    def begin(q):
+        for h in range(2):
+            base = h * HALF + q * SUB
+            for j in range(4):
+                def store(at, value, j=j, base=base):
+                    keep[j, pl.ds(base + at, STEP), :] = value
+
+                add_rows(store, [lambda at, j=j, base=base: keep[j, pl.ds(base + at, STEP), :],
+                                 lambda at, j=j, base=base: rc[j, pl.ds(base + at, STEP), :]], SUB)
+            for copy in first[h, q]:
+                copy.start()
+
+    def pass_on(q):
+        for h in range(2):
+            base = h * HALF + q * SUB
+            for copy in first[h, q]:
+                copy.wait()
+
+            def store(at, value, h=h, base=base):
+                keep[passed[h], pl.ds(base + at, STEP), :] = value
+
+            add_rows(store, [lambda at, h=h, base=base: keep[passed[h], pl.ds(base + at, STEP), :],
+                             lambda at, h=h: r2[h, other[h], pl.ds(q * SUB + at, STEP), :]], SUB)
+            second[h, q].start()
+
+    def along_z(q):
+        for h in range(2):
+            base = h * HALF + q * SUB
+            second[h, q].wait()
+
+            def store(at, value, base=base):
+                acc[pl.ds(base + at, STEP), :] = value
+
+            add_rows(store, [lambda at, base=base: keep[mine, pl.ds(base + at, STEP), :],
+                             lambda at, h=h: r2[h, same[h], pl.ds(q * SUB + at, STEP), :],
+                             lambda at, h=h: r3[h, pl.ds(q * SUB + at, STEP), :]], SUB)
+            for copy in scatter[h, q]:
+                copy.start()
+
+    def share(q):
+        for h in range(2):
+            base = own_rows(h, q)
+            for copy in scatter[h, q]:
+                copy.wait()
+
+            def store(at, value, base=base):
+                cov[pl.ds(base + at, STEP), :] = value
+
+            loads = [lambda at, base=base: acc[pl.ds(base + at, STEP), :]]
+            loads += [lambda at, h=h, d=d: zr[h, q, d, pl.ds(at, STEP), :] for d in range(3)]
+            add_rows(store, loads, ZROWS)
+            for copy in gather[h, q]:
+                copy.start()
+
+    begin(0)
+    pass_on(0)
+    begin(1)
+    along_z(0)
+    pass_on(1)
+    share(0)
+    along_z(1)
+    share(1)
+    for hq in halves:
+        for copy in gather[hq]:
+            copy.wait()
+
+    trio = range(3)
+    width = 3 * BLK
+    sheet = [(lax.broadcasted_iota(jnp.int32, (BLK, width), 0) + BLK * i)
+             == lax.broadcasted_iota(jnp.int32, (BLK, width), 1) for i in trio]
+    rows_of = [pl.ds(BLK * i, BLK) for i in trio]
+
+    def off_part(i, value):
+        return jnp.where(sheet[i], 0.0, value)
+
+    def diag_col(i, value):
+        return jnp.sum(jnp.where(sheet[i], value, 0.0), axis=1, keepdims=True)
+
+    def diag_row(i, value):
+        return jnp.sum(jnp.where(sheet[i], value, 0.0), axis=0, keepdims=True)
+
+    at = 0
+    for i in trio:
+        for j in range(i, 3):
+            block = cov[at * BLK:(at + 1) * BLK, :].astype(jnp.float32)
+            off_a[BLK * i:BLK * (i + 1), BLK * j:BLK * (j + 1)] = block
+            if j > i:
+                off_a[BLK * j:BLK * (j + 1), BLK * i:BLK * (i + 1)] = block.T
+            at += 1
+    col = []
+    row, sums = jnp.zeros((1, width), jnp.float32), jnp.zeros((1, width), jnp.float32)
+    for i in trio:
+        value = off_a[rows_of[i], :]
+        col.append(diag_col(i, value))
+        row = row + diag_row(i, value)
+        sums = sums + jnp.sum(jnp.abs(value), axis=0, keepdims=True)
+    scale = width / jnp.sum(row, axis=1, keepdims=True)
+    limit = jnp.max(sums, axis=1, keepdims=True) * scale + DAMPING
+    shrink = scale / limit
+    a_col = [part * shrink + DAMPING / limit for part in col]
+    a_row = row * shrink + DAMPING / limit
+    for i in trio:
+        value = off_part(i, off_a[rows_of[i], :]) * shrink
+        off_a[rows_of[i], :] = value
+        nar_a[rows_of[i], :] = value.astype(jnp.bfloat16)
+
+    def cross(left_col, left_off, left_nar, right_row, right_off, right_nar, i):
+        value = jnp.dot(left_nar[rows_of[i], :], right_nar[...], preferred_element_type=jnp.float32)
+        return value + left_col[i] * right_off[rows_of[i], :] + left_off[rows_of[i], :] * right_row
+
+    b_col, b_row = [], a_row * a_row
+    for i in trio:
+        value = cross(a_col, off_a, nar_a, a_row, off_a, nar_a, i)
+        b_col.append(a_col[i] * a_col[i] + diag_col(i, value))
+        b_row = b_row + diag_row(i, value)
+        value = off_part(i, value)
+        off_b[rows_of[i], :] = value
+        nar_b[rows_of[i], :] = value.astype(jnp.bfloat16)
+    r_col, y_col = [], []
+    y_row = 4.0 * a_row - 6.0 * b_row + 4.0 * a_row * b_row - b_row * b_row
+    for i in trio:
+        third = cross(a_col, off_a, nar_a, b_row, off_b, nar_b, i)
+        fourth = cross(b_col, off_b, nar_b, b_row, off_b, nar_b, i)
+        fa, fb = off_a[rows_of[i], :], off_b[rows_of[i], :]
+        rest = 4.0 * fb - 6.0 * fa - third
+        prod = 4.0 * fa - 6.0 * fb + 4.0 * third - fourth
+        ac, bc = a_col[i], b_col[i]
+        r_col.append(4.0 * bc - 6.0 * ac - ac * bc + diag_col(i, rest))
+        y_col.append(4.0 * ac - 6.0 * bc + 4.0 * ac * bc - bc * bc + diag_col(i, prod))
+        y_row = y_row + diag_row(i, prod)
+        rest, prod = off_part(i, rest), off_part(i, prod)
+        off_r[rows_of[i], :] = rest
+        off_y[rows_of[i], :] = prod
+        nar_r[rows_of[i], :] = rest.astype(jnp.bfloat16)
+        nar_y[rows_of[i], :] = prod.astype(jnp.bfloat16)
+    inverse_row = jnp.zeros((1, width), jnp.float32)
+    for i in trio:
+        value = cross(r_col, off_r, nar_r, y_row, off_y, nar_y, i)
+        value = 2.0 * off_r[rows_of[i], :] - 4.0 * off_y[rows_of[i], :] - value
+        diag = 8.0 + 2.0 * r_col[i] - 4.0 * y_col[i] - r_col[i] * y_col[i]
+        inverse_row = inverse_row + diag_row(i, value + diag)
+        nar_a[rows_of[i], :] = off_part(i, value / limit).astype(jnp.bfloat16)
+    for f in range(8):
+        @pl.when(4 * core + mine == f)
+        def _(f=f):
+            dall[f] = inverse_row / limit
+
+    local.wait()
+    for (dz, dy), copy in zip(shard_peers, grad_copies):
+        @pl.when(core + y > 0)
+        def _(copy=copy):
+            copy.wait_recv()
+
+        @pl.when(core + y_of[dy] > 0)
+        def _(copy=copy):
+            copy.wait_send()
+
+    weight = weight_of(core, y, x)
+    factor = 4 * core + mine
+    diag_copies = [remote(dall.at[factor], dall.at[factor], ds_.at[i], dr.at[i], (pg, 2 * z + py))
+                   for i, (pg, py) in enumerate(plane_to)]
+    for copy in diag_copies:
+        copy.start()
+    left_copies = [remote(left.at[py], lout.at[weight], ls.at[i], lr.at[i], (pg, 2 * z + py))
+                   for i, (pg, py) in enumerate(plane_to)]
+    input_copies = [remote(nar_a.at[pl.ds(192 * pg, 192)], xout.at[x], ls.at[i], lr.at[i], (pg, 2 * z + py))
+                    for i, (pg, py) in enumerate(plane_to)]
+
+    @pl.when(core + y > 0)
+    def _():
+        for t in range(2):
+            rows = nar_a[pl.ds(pl.multiple_of(z * 192 + t * 96, 16), 96), :]
+            left[t] = jnp.dot(rows, gfull[...], preferred_element_type=jnp.float32).astype(jnp.bfloat16)
+        for copy in left_copies:
+            copy.start()
+        own = pltpu.make_async_copy(left.at[y], lout.at[weight], lsem2)
+        own.start()
+        own.wait()
+        for copy in left_copies:
+            copy.wait_send()
+
+    @pl.when(core + y == 0)
+    def _():
+        for copy in input_copies:
+            copy.start()
+        own = pltpu.make_async_copy(nar_a.at[pl.ds(192 * group, 192)], xout.at[x], lsem2)
+        own.start()
+        own.wait()
+        for copy in input_copies:
+            copy.wait_send()
+
+    for i, (pg, py) in enumerate(plane_from):
+        diag_copies[i].wait()
+
+        @pl.when(lax.rem(pg, 2) + py > 0)
+        def _(i=i):
+            left_copies[i].wait_recv()
+
+        @pl.when(lax.rem(pg, 2) + py == 0)
+        def _(i=i):
+            input_copies[i].wait_recv()
+
+
+def fast_device(hidden, out_grads, global_inputs, query_grads, weight_grads, momentum):
+    width = hidden.shape[1]
+    group, shard, core, x, y, z = position()
+    vmem = pl.BlockSpec(memory_space=pltpu.VMEM)
+    dma = pltpu.SemaphoreType.DMA
+    bf16, f32 = jnp.bfloat16, jnp.float32
+    square, packed = (width, width), (2 * HALF, BLK)
+    left_all, input_all, diag_all = pl.pallas_call(
+        step_kernel,
+        out_shape=(jax.ShapeDtypeStruct((6, 96, width), bf16), jax.ShapeDtypeStruct((2, 192, width), bf16),
+                   jax.ShapeDtypeStruct((8, 1, width), f32)),
+        in_specs=[vmem] * 5,
+        out_specs=(vmem, vmem, vmem),
+        scratch_shapes=[
+            pltpu.VMEM((4,) + packed, bf16), pltpu.VMEM((4,) + packed, bf16), pltpu.VMEM((4,) + packed, bf16),
+            pltpu.VMEM((2, 2, HALF, BLK), bf16), pltpu.VMEM((2, HALF, BLK), bf16), pltpu.VMEM(packed, bf16),
+            pltpu.VMEM((2, PARTS, 3, ZROWS, BLK), bf16), pltpu.VMEM(packed, bf16), pltpu.VMEM(square, bf16),
+        ] + [pltpu.VMEM(square, f32)] * 4 + [pltpu.VMEM(square, bf16)] * 4 + [
+            pltpu.VMEM((2, 96, width), bf16),
+            dma((4,)), dma((4,)), dma((2, PARTS, 2)), dma((2, PARTS, 2)), dma((2, PARTS)), dma((2, PARTS)),
+            dma((2, PARTS, 3)), dma((2, PARTS, 3)), dma((2, PARTS, 3)), dma((2, PARTS, 3)), dma((7,)), dma((7,)),
+            dma((7,)), dma((7,)), dma((7,)), dma((7,)), dma, dma, dma,
+        ],
+        compiler_params=pltpu.CompilerParams(collective_id=0, has_side_effects=True, vmem_limit_bytes=48 * 2**20),
+    )(hidden, global_inputs, out_grads, query_grads, weight_grads)
+    out_diag = lax.dynamic_slice_in_dim(diag_all[2:8, 0], shard * 96, 96, 1)
+    left_side = out_diag[:, :, None] * weight_grads.astype(f32) + left_all.astype(f32)
+    in_diag = lax.dynamic_slice_in_dim(diag_all[0:2, 0], group * 192, 192, 1)
+    columns = lax.dynamic_slice_in_dim(left_side, group * 192, 192, 2)
+    narrow = left_side.astype(bf16)
+
+    def right(rows, which):
+        return lax.dot_general(rows, input_all[which], (((rows.ndim - 1,), (1,)), ((), ())),
+                               preferred_element_type=f32)
+
+    step = jnp.concatenate([
+        right(narrow[0:5], 0) + columns[0:5] * in_diag[0],
+        (right(narrow[5], 1) + columns[5] * in_diag[1])[None],
+    ], axis=0)
+    return MOMENTUM * momentum + step
+
+
 def solution(mesh):
     placed = (
         P(("group", "shard"), None),
@@ -79,6 +466,7 @@
         P(None, "shard", None),
         P(None, "shard", "group"),
     )
+    pairs = mesh.shape["group"] == 4 and mesh.shape["shard"] == 8
     return jax.shard_map(
-        on_device, mesh=mesh, in_specs=placed, out_specs=P(None, "shard", "group"), check_vma=False
+        fast_device if pairs else on_device, mesh=mesh, in_specs=placed, out_specs=P(None, "shard", "group"), check_vma=False
     )

time: 534 us -> 102 us (0.19)
  waiting for transfers between devices: 207 us -> 0 us
  blocking collectives: 186 us -> 0 us
  matrix products: 101 us -> 0.63 us
  Pallas kernels: 0 us -> 93.9 us
  between operations: 15.5 us -> 0.06 us
  other arithmetic: 14.3 us -> 1.23 us
    psum x1 -> x0, blocking collectives: 186 us -> none  [on_device(): factor_full = lax.psum(summed, 'shard')]
    dot_general x17 -> x2, matrix products: 101 us -> 0.63 us  [right(): lax.dot_general(rows, input_all[which], (((rows.ndim - 1,), (1,)), ((), (...]
    pallas_call x0 -> x1, Pallas kernels: none -> 93.9 us  [fast_device(): pl.pallas_call(step_kernel, out_shape=(jax.ShapeDtypeStruct((6, 96, width...]
    psum x1 -> x0, waiting for transfers between devices: 90.4 us -> none  [broadcast(): return lax.psum(jnp.where(mine, array, jnp.zeros_like(array)), axis)]
    reduce_scatter x1 -> x0, waiting for transfers between devices: 77.7 us -> none  [on_device(): lax.psum_scatter(stacked, 'group', scatter_dimension=0, tiled=True)]
    all_gather x2 -> x0, waiting for transfers between devices: 38.7 us -> none  [the longest x1 26.9 us: on_device(): all_rows = lax.all_gather(own_rows, 'group', axis=0, tiled=True)]
    reduce_sum x2 -> x0, other arithmetic: 6.64 us -> none  [the longest x1 3.66 us: on_device(): mean_diag = jnp.trace(covariance, axis1=1, axis2=2) / model_width]
  transfers between devices with their start and end apart: 4 -> 0, of which waited for: 4 -> 0; matrix products, arithmetic and copies ran while one was open for 1% -> 0% of each run, Pallas kernels for 0% -> 0%
where the time goes in v2:
time: 102 us
  Pallas kernels  93.9 us (92%)
  local copies, waits for them, and re-layouts  5.89 us (6%)
  other arithmetic  1.23 us (1%)
    pallas_call x1, Pallas kernels, fast_device(): pl.pallas_call(step_kernel, out_shape=(jax.ShapeDtypeStruct((6, 96, width...  93.9 us
    unnamed x13, local copies, waits for them, and re-layouts  5.72 us

profile of v2, /device:TPU:13, one launch (start us, length us, event | category | flops | bytes accessed | tf_op | source)
XLA Modules:
  0.0 101.7 jit_solution(5382028744088918537)
XLA Ops:
  0.0 0.0 copy-start
  0.0 1.2 %copy-done = bf16[6,96,768]{2,1,0:T(8,128)(2,1)S(1)} copy-done((bf16[6,96,768]{2,1,0:T(8,128)(2,1)S(1)}, bf16[6,96,768]{2,1,0:T(8,128)(2,1)}, u32[]{:S(2)}) %copy-start) | copy-done | bytes 884760
  1.2 0.0 copy-start.1
  1.2 1.5 %copy-done.1 = bf16[5,256,768]{2,1,0:T(8,128)(2,1)S(1)} copy-done((bf16[5,256,768]{2,1,0:T(8,128)(2,1)S(1)}, bf16[5,256,768]{2,1,0:T(8,128)(2,1)}, u32[]{:S(2)}) %copy-start.1) | copy-done | bytes 1966104
  2.7 0.0 copy-start.2
  2.7 1.0 copy-done.2
  3.7 0.0 copy-start.3
  3.7 0.8 copy-done.3
  4.5 0.0 copy-start.4
  4.5 0.8 copy-done.4
  5.3 93.9 %shard_map.64 = (bf16[6,96,768]{2,1,0:T(8,128)(2,1)S(1)}, bf16[2,192,768]{2,1,0:T(8,128)(2,1)S(1)}, f32[8,1,768]{2,1,0:T(1,128)S(1)}) custom-call(bf16[256,768]{1,0:T(8,128)(2,1)S(1)} %copy-done.2, bf16[32,768]{1,0:T(8,128)(2,1)S(1)} %copy-done.3, bf16[5,256,768]{2,1,0:T(8,128)(2,1)S(1)} %copy-done.1, bf16[32,768]{1,0:T(8,128)(2,1)S(1)} %copy-done.4, ...), custom_call_target="tpu_custom_call" | custom-call | tf_op jit(solution)/shard_map/pallas_call | solution.py:425
  99.3 0.1 constant_dynamic-slice_fusion.2
  99.4 0.1 constant_dynamic-slice_fusion
  99.4 0.3 fusion.6
  99.8 0.0 copy-start.5
  99.8 0.2 fusion
  100.0 0.4 convolution_add_fusion
  100.4 0.4 copy-done.5
  100.8 0.9 maximum_add_fusion
  (3 shorter events, 0.0 us)
Async XLA Ops:
  0.0 1.2 %copy-start = (bf16[6,96,768]{2,1,0:T(8,128)(2,1)S(1)}, bf16[6,96,768]{2,1,0:T(8,128)(2,1)}, u32[]{:S(2)}) copy-start(bf16[6,96,768]{2,1,0:T(8,128)(2,1)} %wgr.1) | copy-start | bytes 2654212
  1.2 1.5 %copy-start.1 = (bf16[5,256,768]{2,1,0:T(8,128)(2,1)S(1)}, bf16[5,256,768]{2,1,0:T(8,128)(2,1)}, u32[]{:S(2)}) copy-start(bf16[5,256,768]{2,1,0:T(8,128)(2,1)} %outg.1) | copy-start | bytes 5898244
  2.7 1.0 copy-start.2
  3.7 0.8 copy-start.3
  4.5 0.8 copy-start.4
  99.8 1.1 %copy-start.5 = (f32[6,96,192]{2,1,0:T(8,128)S(1)}, f32[6,96,192]{2,1,0:T(8,128)}, u32[]{:S(2)}) copy-start(f32[6,96,192]{2,1,0:T(8,128)} %param.11) | copy-start | bytes 1327108

commit v3 on v2

--- a/solution.py
+++ b/solution.py
@@ -75,10 +75,9 @@
 MESH = pl.DeviceIdType.MESH
 BLK = 256
 HALF = 768
-PARTS = 2
-SUB = HALF // PARTS
-ZROWS = SUB // 4
+PARTS = 3
 STEP = 32
+FACTOR_AT = (0, 3, 2, 1, 4, 5, 6, 7)
 
 
 def position():
@@ -89,7 +88,11 @@
 
 
 def weight_of(core, y, x):
-    return core * (2 + 2 * y + x) + (1 - core) * y * x
+    return core * (2 + 2 * y + x) + (1 - core) * (1 - y)
+
+
+def kind_of(core, y, x):
+    return core + (x - y) * (x - y)
 
 
 def greet(peers):
@@ -111,9 +114,9 @@
     lax.fori_loop(0, rows // STEP, step, 0)
 
 
-def step_kernel(hid, ginp, outg, qry, wgr, lout, xout, dall, sendb, keep, rc, r2, r3, acc, zr,
-                cov, gfull, off_a, off_b, off_r, off_y, nar_a, nar_b, nar_r, nar_y, left,
-                cs, cr, as_, ar, bs, br, zs, zrs, fs, fr, gs, gr, ls, lr, ds_, dr, lsem, lsem2, dsem):
+def step_kernel(hid, ginp, outg, qry, wgr, lout, xout, dall, hidv, ginpv, outgv, qryv, sendb, keep, rc, r2, r3, acc,
+                zr1, zr2, cov, gfull, off_a, off_b, off_r, off_y, nar_a, nar_b, nar_r, nar_y, left,
+                cs, cr, as_, ar, bs, br, zs, zrs, fs, fr, gs, gr, ls, lr, ds_, dr, is_, ir, rs, ins, lsem, lsem2):
     group, shard, core, x, y, z = position()
     sibling = (group + 1 - 2 * core, shard)
     x_peer = ((1 - x) * 2 + core, shard)
@@ -125,6 +128,11 @@
     plane_to = [(lax.rem(group + dg, 4), y_of[dy]) for dg, dy in plane]
     plane_from = [(lax.rem(group + 4 - dg, 4), y_of[dy]) for dg, dy in plane]
     outside = [(pg, 2 * z + py) for (pg, py), (dg, dy) in zip(plane_to, plane) if dg > 0]
+    loads = [pltpu.make_async_copy(hid, hidv, ins.at[0]), pltpu.make_async_copy(ginp, ginpv, ins.at[1])]
+    loads += [pltpu.make_async_copy(outg.at[i], outgv.at[i], ins.at[2 + i]) for i in range(5)]
+    loads += [pltpu.make_async_copy(qry, qryv, ins.at[7])]
+    for i in (4, 5, 6, 7, 0, 1, 2, 3):
+        loads[i].start()
     greet(outside + [(group, 2 * z_of[dz] + y_of[dy]) for dz, dy in shard_peers])
 
     def remote(src, dst, send, recv, device):
@@ -133,14 +141,15 @@
         )
 
     def partial(factor, dst):
+        loads[factor].wait()
         if factor == 0:
-            rows = hid[...]
+            rows = hidv[...]
         elif factor == 1:
-            rows = ginp[...]
+            rows = ginpv[...]
         elif factor == 7:
-            rows = qry[...]
+            rows = qryv[...]
         else:
-            rows = outg[factor - 2]
+            rows = outgv[factor - 2]
         at = 0
         for i in range(3):
             prod = lax.dot_general(
@@ -156,77 +165,80 @@
         grad_copies.append(remote(wgr.at[weight_of(core, y_of[dy], x)], gfull.at[pl.ds(shard * 96, 96)], gs.at[i],
                                   gr.at[i], (group, 2 * z_of[dz] + y_of[dy])))
 
-        @pl.when(core + y_of[dy] > 0)
+        @pl.when(kind_of(core, y_of[dy], x) > 0)
         def _(copy=grad_copies[-1]):
             copy.start()
 
     local = pltpu.make_async_copy(wgr.at[weight_of(core, y, x)], gfull.at[pl.ds(shard * 96, 96)], lsem)
     local.start()
-    core_copies = [remote(sendb.at[j], rc.at[j], cs.at[j], cr.at[j], sibling) for j in range(4)]
+    core_copies = [[remote(sendb.at[j, pl.ds(512 * q, 512)], rc.at[j, pl.ds(512 * q, 512)], cs.at[j, q], cr.at[j, q],
+                           sibling) for q in range(PARTS)] for j in range(4)]
     for owner in range(2):
         @pl.when(core != owner)
         def _():
             for j in range(4):
-                partial(4 * owner + j, sendb.at[j])
-                core_copies[j].start()
+                partial(FACTOR_AT[4 * owner + j], sendb.at[j])
+                core_copies[j][0].start()
+            for q in range(1, PARTS):
+                for j in range(4):
+                    core_copies[j][q].start()
 
     for owner in range(2):
         @pl.when(core == owner)
         def _():
             for j in range(4):
-                partial(4 * owner + j, keep.at[j])
-
-    for j in range(4):
-        core_copies[j].wait()
-
-    def first_of(h, q):
-        rows = pl.ds(h * HALF + q * SUB, SUB)
-        into = pl.ds(q * SUB, SUB)
-        if h == 0:
-            return [remote(keep.at[2 * t + 1 - x, rows], r2.at[0, t, into], as_.at[h, q, t], ar.at[h, q, t], x_peer)
-                    for t in range(2)]
-        return [remote(keep.at[2 * (1 - y) + t, rows], r2.at[1, t, into], as_.at[h, q, t], ar.at[h, q, t], y_peer)
-                for t in range(2)]
+                partial(FACTOR_AT[4 * owner + j], keep.at[j])
 
     passed = [2 * (1 - y) + x, 2 * y + 1 - x]
     other = [1 - y, 1 - x]
     same = [y, x]
     mine = 2 * y + x
+    zh, zl = z // 2, lax.rem(z, 2)
+    near = (group, 2 * (z + 1 - 2 * zl) + y)
+    far = (group, 2 * (z + 2 - 4 * zh) + y)
+
+    def first_of(h, q):
+        rows = pl.ds(512 * q + BLK * h, BLK)
+        if h == 0:
+            return [remote(keep.at[2 * t + 1 - x, rows], r2.at[0, q, t], as_.at[h, q, t], ar.at[h, q, t], x_peer)
+                    for t in range(2)]
+        return [remote(keep.at[2 * (1 - y) + t, rows], r2.at[1, q, t], as_.at[h, q, t], ar.at[h, q, t], y_peer)
+                for t in range(2)]
+
     halves = [(h, q) for q in range(PARTS) for h in range(2)]
     first = {hq: first_of(*hq) for hq in halves}
-    second = {(h, q): remote(keep.at[passed[h], pl.ds(h * HALF + q * SUB, SUB)], r3.at[h, pl.ds(q * SUB, SUB)],
+    second = {(h, q): remote(keep.at[passed[h], pl.ds(512 * q + BLK * h, BLK)], r3.at[h, q],
                              bs.at[h, q], br.at[h, q], [y_peer, x_peer][h]) for h, q in halves}
 
-    def own_rows(h, q):
-        return h * HALF + q * SUB + z * ZROWS
-
-    def scatter_of(h, q):
-        return [remote(acc.at[pl.ds(h * HALF + q * SUB + z_of[dz] * ZROWS, ZROWS)], zr.at[h, q, dz - 1],
-                       zs.at[h, q, dz - 1], zrs.at[h, q, dz - 1], (group, 2 * z_of[dz] + y)) for dz in range(1, 4)]
-
-    def gather_of(h, q):
-        rows = pl.ds(own_rows(h, q), ZROWS)
-        return [remote(cov.at[rows], cov.at[rows], fs.at[h, q, dz - 1], fr.at[h, q, dz - 1],
-                       (group, 2 * z_of[dz] + y)) for dz in range(1, 4)]
-
-    scatter = {hq: scatter_of(*hq) for hq in halves}
-    gather = {hq: gather_of(*hq) for hq in halves}
+    def quarter(q):
+        return 512 * q + 256 * zl + 128 * zh
+
+    halve = [remote(acc.at[pl.ds(512 * q + 256 * (1 - zl), 256)], zr1.at[q], zs.at[0, q], zrs.at[0, q], near)
+             for q in range(PARTS)]
+    halve2 = [remote(acc.at[pl.ds(512 * q + 256 * zl + 128 * (1 - zh), 128)], zr2.at[q], zs.at[1, q], zrs.at[1, q],
+                     far) for q in range(PARTS)]
+    double = [remote(cov.at[pl.ds(quarter(q), 128)], cov.at[pl.ds(quarter(q), 128)], fs.at[0, q], fr.at[0, q], far)
+              for q in range(PARTS)]
+    double2 = [remote(cov.at[pl.ds(512 * q + 256 * zl, 256)], cov.at[pl.ds(512 * q + 256 * zl, 256)], fs.at[1, q],
+                      fr.at[1, q], near) for q in range(PARTS)]
 
     def begin(q):
-        for h in range(2):
-            base = h * HALF + q * SUB
-            for j in range(4):
-                def store(at, value, j=j, base=base):
-                    keep[j, pl.ds(base + at, STEP), :] = value
-
-                add_rows(store, [lambda at, j=j, base=base: keep[j, pl.ds(base + at, STEP), :],
-                                 lambda at, j=j, base=base: rc[j, pl.ds(base + at, STEP), :]], SUB)
-            for copy in first[h, q]:
-                copy.start()
+        base = 512 * q
+        for j in range(4):
+            core_copies[j][q].wait()
+
+            def store(at, value, j=j):
+                keep[j, pl.ds(base + at, STEP), :] = value
+
+            add_rows(store, [lambda at, j=j: keep[j, pl.ds(base + at, STEP), :],
+                             lambda at, j=j: rc[j, pl.ds(base + at, STEP), :]], 512)
+        for t in range(2):
+            for h in range(2):
+                first[h, q][t].start()
 
     def pass_on(q):
         for h in range(2):
-            base = h * HALF + q * SUB
+            base = 512 * q + BLK * h
             for copy in first[h, q]:
                 copy.wait()
 
@@ -234,49 +246,53 @@
                 keep[passed[h], pl.ds(base + at, STEP), :] = value
 
             add_rows(store, [lambda at, h=h, base=base: keep[passed[h], pl.ds(base + at, STEP), :],
-                             lambda at, h=h: r2[h, other[h], pl.ds(q * SUB + at, STEP), :]], SUB)
+                             lambda at, h=h: r2[h, q, other[h], pl.ds(at, STEP), :]], BLK)
             second[h, q].start()
 
-    def along_z(q):
+    def z_near(q):
         for h in range(2):
-            base = h * HALF + q * SUB
+            base = 512 * q + BLK * h
             second[h, q].wait()
 
             def store(at, value, base=base):
                 acc[pl.ds(base + at, STEP), :] = value
 
             add_rows(store, [lambda at, base=base: keep[mine, pl.ds(base + at, STEP), :],
-                             lambda at, h=h: r2[h, same[h], pl.ds(q * SUB + at, STEP), :],
-                             lambda at, h=h: r3[h, pl.ds(q * SUB + at, STEP), :]], SUB)
-            for copy in scatter[h, q]:
-                copy.start()
-
-    def share(q):
-        for h in range(2):
-            base = own_rows(h, q)
-            for copy in scatter[h, q]:
-                copy.wait()
-
-            def store(at, value, base=base):
-                cov[pl.ds(base + at, STEP), :] = value
-
-            loads = [lambda at, base=base: acc[pl.ds(base + at, STEP), :]]
-            loads += [lambda at, h=h, d=d: zr[h, q, d, pl.ds(at, STEP), :] for d in range(3)]
-            add_rows(store, loads, ZROWS)
-            for copy in gather[h, q]:
-                copy.start()
-
-    begin(0)
-    pass_on(0)
-    begin(1)
-    along_z(0)
-    pass_on(1)
-    share(0)
-    along_z(1)
-    share(1)
-    for hq in halves:
-        for copy in gather[hq]:
-            copy.wait()
+                             lambda at, h=h: r2[h, q, same[h], pl.ds(at, STEP), :],
+                             lambda at, h=h: r3[h, q, pl.ds(at, STEP), :]], BLK)
+        halve[q].start()
+
+    def z_far(q):
+        base = 512 * q + 256 * zl
+        halve[q].wait()
+
+        def store(at, value):
+            acc[pl.ds(base + at, STEP), :] = value
+
+        add_rows(store, [lambda at: acc[pl.ds(base + at, STEP), :], lambda at: zr1[q, pl.ds(at, STEP), :]], 256)
+        halve2[q].start()
+
+    def back_far(q):
+        base = quarter(q)
+        halve2[q].wait()
+
+        def store(at, value):
+            cov[pl.ds(base + at, STEP), :] = value
+
+        add_rows(store, [lambda at: acc[pl.ds(base + at, STEP), :], lambda at: zr2[q, pl.ds(at, STEP), :]], 128)
+        double[q].start()
+
+    def back_near(q):
+        double[q].wait()
+        double2[q].start()
+
+    stages = [begin, pass_on, z_near, z_far, back_far, back_near]
+    for tick in range(PARTS + len(stages) - 1):
+        for depth in reversed(range(len(stages))):
+            if 0 <= tick - depth < PARTS:
+                stages[depth](tick - depth)
+    for copy in double2:
+        copy.wait()
 
     trio = range(3)
     width = 3 * BLK
@@ -361,11 +377,11 @@
 
     local.wait()
     for (dz, dy), copy in zip(shard_peers, grad_copies):
-        @pl.when(core + y > 0)
+        @pl.when(kind_of(core, y, x) > 0)
         def _(copy=copy):
             copy.wait_recv()
 
-        @pl.when(core + y_of[dy] > 0)
+        @pl.when(kind_of(core, y_of[dy], x) > 0)
         def _(copy=copy):
             copy.wait_send()
 
@@ -377,10 +393,12 @@
         copy.start()
     left_copies = [remote(left.at[py], lout.at[weight], ls.at[i], lr.at[i], (pg, 2 * z + py))
                    for i, (pg, py) in enumerate(plane_to)]
-    input_copies = [remote(nar_a.at[pl.ds(192 * pg, 192)], xout.at[x], ls.at[i], lr.at[i], (pg, 2 * z + py))
-                    for i, (pg, py) in enumerate(plane_to)]
-
-    @pl.when(core + y > 0)
+    straight = [(i, pg, py) for i, (pg, py) in enumerate(plane_to)]
+    input_copies = [remote(nar_a.at[pl.ds(192 * pg, 192)], xout.at[y], is_.at[i], ir.at[y], (pg, 2 * z + py))
+                    for i, pg, py in straight]
+    relay = remote(xout.at[y], xout.at[y], rs, ir.at[y], y_peer)
+
+    @pl.when(kind_of(core, y, x) > 0)
     def _():
         for t in range(2):
             rows = nar_a[pl.ds(pl.multiple_of(z * 192 + t * 96, 16), 96), :]
@@ -390,29 +408,53 @@
         own = pltpu.make_async_copy(left.at[y], lout.at[weight], lsem2)
         own.start()
         own.wait()
+
+    def to_straight(act):
+        for copy, (i, pg, py) in zip(input_copies, straight):
+            @pl.when((pg // 2 - x) * (py - y) == 0)
+            def _(copy=copy):
+                act(copy)
+
+    @pl.when(kind_of(core, y, x) == 0)
+    def _():
+        to_straight(lambda copy: copy.start())
+        own = pltpu.make_async_copy(nar_a.at[pl.ds(192 * group, 192)], xout.at[y], lsem2)
+        own.start()
+        own.wait()
+
+    def arrived(which):
+        remote(xout.at[which], xout.at[which], rs, ir.at[which], y_peer).wait_recv()
+
+    @pl.when((x - y) * (x - y) > 0)
+    def _():
+        arrived(y)
+        relay.start()
+        arrived(1 - y)
+        relay.wait_send()
+
+    @pl.when((x - y) * (x - y) == 0)
+    def _():
+        arrived(1 - y)
+
+        @pl.when(core > 0)
+        def _():
+            arrived(y)
+
+    @pl.when(kind_of(core, y, x) > 0)
+    def _():
         for copy in left_copies:
             copy.wait_send()
 
-    @pl.when(core + y == 0)
+    @pl.when(kind_of(core, y, x) == 0)
     def _():
-        for copy in input_copies:
-            copy.start()
-        own = pltpu.make_async_copy(nar_a.at[pl.ds(192 * group, 192)], xout.at[x], lsem2)
-        own.start()
-        own.wait()
-        for copy in input_copies:
-            copy.wait_send()
+        to_straight(lambda copy: copy.wait_send())
 
     for i, (pg, py) in enumerate(plane_from):
         diag_copies[i].wait()
 
-        @pl.when(lax.rem(pg, 2) + py > 0)
+        @pl.when(kind_of(lax.rem(pg, 2), py, pg // 2) > 0)
         def _(i=i):
             left_copies[i].wait_recv()
-
-        @pl.when(lax.rem(pg, 2) + py == 0)
-        def _(i=i):
-            input_copies[i].wait_recv()
 
 
 def fast_device(hidden, out_grads, global_inputs, query_grads, weight_grads, momentum):
@@ -426,23 +468,26 @@
         step_kernel,
         out_shape=(jax.ShapeDtypeStruct((6, 96, width), bf16), jax.ShapeDtypeStruct((2, 192, width), bf16),
                    jax.ShapeDtypeStruct((8, 1, width), f32)),
-        in_specs=[vmem] * 5,
+        in_specs=[pl.BlockSpec(memory_space=pltpu.HBM)] * 5,
         out_specs=(vmem, vmem, vmem),
         scratch_shapes=[
+            pltpu.VMEM(hidden.shape, bf16), pltpu.VMEM(global_inputs.shape, bf16),
+            pltpu.VMEM(out_grads.shape, bf16), pltpu.VMEM(query_grads.shape, bf16),
             pltpu.VMEM((4,) + packed, bf16), pltpu.VMEM((4,) + packed, bf16), pltpu.VMEM((4,) + packed, bf16),
-            pltpu.VMEM((2, 2, HALF, BLK), bf16), pltpu.VMEM((2, HALF, BLK), bf16), pltpu.VMEM(packed, bf16),
-            pltpu.VMEM((2, PARTS, 3, ZROWS, BLK), bf16), pltpu.VMEM(packed, bf16), pltpu.VMEM(square, bf16),
+            pltpu.VMEM((2, PARTS, 2, BLK, BLK), bf16), pltpu.VMEM((2, PARTS, BLK, BLK), bf16),
+            pltpu.VMEM(packed, bf16), pltpu.VMEM((PARTS, 256, BLK), bf16), pltpu.VMEM((PARTS, 128, BLK), bf16),
+            pltpu.VMEM(packed, bf16), pltpu.VMEM(square, bf16),
         ] + [pltpu.VMEM(square, f32)] * 4 + [pltpu.VMEM(square, bf16)] * 4 + [
             pltpu.VMEM((2, 96, width), bf16),
-            dma((4,)), dma((4,)), dma((2, PARTS, 2)), dma((2, PARTS, 2)), dma((2, PARTS)), dma((2, PARTS)),
-            dma((2, PARTS, 3)), dma((2, PARTS, 3)), dma((2, PARTS, 3)), dma((2, PARTS, 3)), dma((7,)), dma((7,)),
-            dma((7,)), dma((7,)), dma((7,)), dma((7,)), dma, dma, dma,
+            dma((4, PARTS)), dma((4, PARTS)), dma((2, PARTS, 2)), dma((2, PARTS, 2)), dma((2, PARTS)),
+            dma((2, PARTS)), dma((2, PARTS)), dma((2, PARTS)), dma((2, PARTS)), dma((2, PARTS)), dma((7,)), dma((7,)),
+            dma((7,)), dma((7,)), dma((7,)), dma((7,)), dma((7,)), dma((2,)), dma, dma((8,)), dma, dma,
         ],
         compiler_params=pltpu.CompilerParams(collective_id=0, has_side_effects=True, vmem_limit_bytes=48 * 2**20),
     )(hidden, global_inputs, out_grads, query_grads, weight_grads)
-    out_diag = lax.dynamic_slice_in_dim(diag_all[2:8, 0], shard * 96, 96, 1)
+    out_diag = lax.dynamic_slice_in_dim(jnp.stack([diag_all[i, 0] for i in (2, 1, 4, 5, 6, 7)]), shard * 96, 96, 1)
     left_side = out_diag[:, :, None] * weight_grads.astype(f32) + left_all.astype(f32)
-    in_diag = lax.dynamic_slice_in_dim(diag_all[0:2, 0], group * 192, 192, 1)
+    in_diag = lax.dynamic_slice_in_dim(jnp.stack([diag_all[i, 0] for i in (0, 3)]), group * 192, 192, 1)
     columns = lax.dynamic_slice_in_dim(left_side, group * 192, 192, 2)
     narrow = left_side.astype(bf16)
 

time: 102 us -> 102 us (level)
  the two profiles are of different devices: /device:TPU:13 before, /device:TPU:1 now
where the time goes in v3:
time: 102 us; the launch traced here: 101 us
  Pallas kernels  93.6 us (92%)
  local copies, waits for them, and re-layouts  5.86 us (6%)
  other arithmetic  1.31 us (1%)
    pallas_call x1, Pallas kernels, fast_device(): pl.pallas_call(step_kernel, out_shape=(jax.ShapeDtypeStruct((6, 96, width...  93.6 us
    unnamed x14, local copies, waits for them, and re-layouts  5.72 us

profile of v3, /device:TPU:1, one launch (start us, length us, event | category | flops | bytes accessed | tf_op | source)
XLA Modules:
  0.0 101.5 jit_solution(15992882071517181957)
XLA Ops:
  0.0 0.0 copy-start
  0.0 1.2 %copy-done = bf16[6,96,768]{2,1,0:T(8,128)(2,1)S(1)} copy-done((bf16[6,96,768]{2,1,0:T(8,128)(2,1)S(1)}, bf16[6,96,768]{2,1,0:T(8,128)(2,1)}, u32[]{:S(2)}) %copy-start) | copy-done | bytes 884760
  1.2 0.0 copy-start.2
  1.2 1.5 %copy-done.2 = bf16[5,256,768]{2,1,0:T(8,128)(2,1)S(1)} copy-done((bf16[5,256,768]{2,1,0:T(8,128)(2,1)S(1)}, bf16[5,256,768]{2,1,0:T(8,128)(2,1)}, u32[]{:S(2)}) %copy-start.2) | copy-done | bytes 1966104
  2.7 0.0 copy-start.3
  2.7 1.0 copy-done.3
  3.7 0.0 copy-start.4
  3.7 0.8 copy-done.4
  4.5 0.0 copy-start.5
  4.5 0.8 copy-done.5
  5.3 0.0 copy-start.1
  5.3 93.6 %shard_map.64 = (bf16[6,96,768]{2,1,0:T(8,128)(2,1)S(1)}, bf16[2,192,768]{2,1,0:T(8,128)(2,1)S(1)}, f32[8,1,768]{2,1,0:T(1,128)S(1)}) custom-call(bf16[256,768]{1,0:T(8,128)(2,1)S(1)} %copy-done.3, bf16[32,768]{1,0:T(8,128)(2,1)S(1)} %copy-done.4, bf16[5,256,768]{2,1,0:T(8,128)(2,1)S(1)} %copy-done.2, bf16[32,768]{1,0:T(8,128)(2,1)S(1)} %copy-done.5, ...), custom_call_target="tpu_custom_call" | custom-call | tf_op jit(solution)/shard_map/pallas_call | solution.py:467
  98.9 0.1 fusion.6
  99.1 0.1 constant_dynamic-slice_fusion
  99.2 0.0 copy-done.1
  99.2 0.3 fusion.7
  99.5 0.0 copy-start.6
  99.5 0.2 fusion
  99.7 0.4 convolution_add_fusion
  100.1 0.4 copy-done.6
  100.6 0.9 maximum_add_fusion
  (3 shorter events, 0.1 us)
Async XLA Ops:
  0.0 1.2 %copy-start = (bf16[6,96,768]{2,1,0:T(8,128)(2,1)S(1)}, bf16[6,96,768]{2,1,0:T(8,128)(2,1)}, u32[]{:S(2)}) copy-start(bf16[6,96,768]{2,1,0:T(8,128)(2,1)} %wgr.1) | copy-start | bytes 2654212
  1.2 1.5 %copy-start.2 = (bf16[5,256,768]{2,1,0:T(8,128)(2,1)S(1)}, bf16[5,256,768]{2,1,0:T(8,128)(2,1)}, u32[]{:S(2)}) copy-start(bf16[5,256,768]{2,1,0:T(8,128)(2,1)} %outg.1) | copy-start | bytes 5898244
  2.7 1.0 copy-start.3
  3.7 0.8 copy-start.4
  4.5 0.8 copy-start.5
  5.3 93.8 %copy-start.1 = (bf16[6,96,768]{2,1,0:T(8,128)(2,1)S(1)}, bf16[6,96,768]{2,1,0:T(8,128)(2,1)}, u32[]{:S(2)}) copy-start(bf16[6,96,768]{2,1,0:T(8,128)(2,1)} %wgr.1) | copy-start | bytes 2654212
  99.5 1.1 %copy-start.6 = (f32[6,96,192]{2,1,0:T(8,128)S(1)}, f32[6,96,192]{2,1,0:T(8,128)}, u32[]{:S(2)}) copy-start(f32[6,96,192]{2,1,0:T(8,128)} %param.11) | copy-start | bytes 1327108

commit v4 on v3

--- a/solution.py
+++ b/solution.py
@@ -288,7 +288,7 @@
 
     stages = [begin, pass_on, z_near, z_far, back_far, back_near]
     for tick in range(PARTS + len(stages) - 1):
-        for depth in reversed(range(len(stages))):
+        for depth in range(len(stages)):
             if 0 <= tick - depth < PARTS:
                 stages[depth](tick - depth)
     for copy in double2:

time: 102 us -> 103 us (level)
  Pallas kernels: 93.6 us -> 95.2 us
    pallas_call x1, Pallas kernels: 93.6 us -> 95.2 us  [fast_device(): pl.pallas_call(step_kernel, out_shape=(jax.ShapeDtypeStruct((6, 96, width...]
where the time goes in v4:
time: 103 us
  Pallas kernels  95.2 us (92%)
  local copies, waits for them, and re-layouts  5.86 us (6%)
  other arithmetic  1.31 us (1%)
    pallas_call x1, Pallas kernels, fast_device(): pl.pallas_call(step_kernel, out_shape=(jax.ShapeDtypeStruct((6, 96, width...  95.2 us
    unnamed x14, local copies, waits for them, and re-layouts  5.72 us

profile of v4, /device:TPU:1, one launch (start us, length us, event | category | flops | bytes accessed | tf_op | source)
XLA Modules:
  0.0 103.0 jit_solution(15199495032779451711)
XLA Ops:
  0.0 0.0 copy-start
  0.0 1.2 %copy-done = bf16[6,96,768]{2,1,0:T(8,128)(2,1)S(1)} copy-done((bf16[6,96,768]{2,1,0:T(8,128)(2,1)S(1)}, bf16[6,96,768]{2,1,0:T(8,128)(2,1)}, u32[]{:S(2)}) %copy-start) | copy-done | bytes 884760
  1.2 0.0 copy-start.2
  1.2 1.5 %copy-done.2 = bf16[5,256,768]{2,1,0:T(8,128)(2,1)S(1)} copy-done((bf16[5,256,768]{2,1,0:T(8,128)(2,1)S(1)}, bf16[5,256,768]{2,1,0:T(8,128)(2,1)}, u32[]{:S(2)}) %copy-start.2) | copy-done | bytes 1966104
  2.7 0.0 copy-start.3
  2.7 1.0 copy-done.3
  3.7 0.0 copy-start.4
  3.7 0.8 copy-done.4
  4.5 0.0 copy-start.5
  4.5 0.8 copy-done.5
  5.3 0.0 copy-start.1
  5.3 95.2 %shard_map.64 = (bf16[6,96,768]{2,1,0:T(8,128)(2,1)S(1)}, bf16[2,192,768]{2,1,0:T(8,128)(2,1)S(1)}, f32[8,1,768]{2,1,0:T(1,128)S(1)}) custom-call(bf16[256,768]{1,0:T(8,128)(2,1)S(1)} %copy-done.3, bf16[32,768]{1,0:T(8,128)(2,1)S(1)} %copy-done.4, bf16[5,256,768]{2,1,0:T(8,128)(2,1)S(1)} %copy-done.2, bf16[32,768]{1,0:T(8,128)(2,1)S(1)} %copy-done.5, ...), custom_call_target="tpu_custom_call" | custom-call | tf_op jit(solution)/shard_map/pallas_call | solution.py:467
  100.5 0.1 fusion.6
  100.6 0.1 constant_dynamic-slice_fusion
  100.7 0.0 copy-done.1
  100.7 0.3 fusion.7
  101.1 0.0 copy-start.6
  101.1 0.2 fusion
  101.3 0.4 convolution_add_fusion
  101.7 0.4 copy-done.6
  102.1 0.9 maximum_add_fusion
  (3 shorter events, 0.1 us)
Async XLA Ops:
  0.0 1.2 %copy-start = (bf16[6,96,768]{2,1,0:T(8,128)(2,1)S(1)}, bf16[6,96,768]{2,1,0:T(8,128)(2,1)}, u32[]{:S(2)}) copy-start(bf16[6,96,768]{2,1,0:T(8,128)(2,1)} %wgr.1) | copy-start | bytes 2654212
  1.2 1.5 %copy-start.2 = (bf16[5,256,768]{2,1,0:T(8,128)(2,1)S(1)}, bf16[5,256,768]{2,1,0:T(8,128)(2,1)}, u32[]{:S(2)}) copy-start(bf16[5,256,768]{2,1,0:T(8,128)(2,1)} %outg.1) | copy-start | bytes 5898244
  2.7 1.0 copy-start.3
  3.7 0.8 copy-start.4
  4.5 0.8 copy-start.5
  5.3 95.4 %copy-start.1 = (bf16[6,96,768]{2,1,0:T(8,128)(2,1)S(1)}, bf16[6,96,768]{2,1,0:T(8,128)(2,1)}, u32[]{:S(2)}) copy-start(bf16[6,96,768]{2,1,0:T(8,128)(2,1)} %wgr.1) | copy-start | bytes 2654212
  101.1 1.1 %copy-start.6 = (f32[6,96,192]{2,1,0:T(8,128)S(1)}, f32[6,96,192]{2,1,0:T(8,128)}, u32[]{:S(2)}) copy-start(f32[6,96,192]{2,1,0:T(8,128)} %param.11) | copy-start | bytes 1327108
